TPU v7x, 32 devices: a whole 2x2x4 slice. The times are simulated.
32 devices in a mesh: shard: 16 (over z, x, core), rep: 2 (over y).
Axes of the slice: x: 2, y: 2, z: 4, core: 2. Of those that a mesh axis runs over, the one named last changes fastest.
Arguments:
- frames: bfloat16 [32, 256, 768], P(('shard', 'rep')), may hold values from -6 to 6
- cotangent: bfloat16 [32, 256, 768], P(('shard', 'rep')), may hold values from -6 to 6
- first_gain: bfloat16 [768], P('shard'), may hold values from 0.5 to 1.5
- first_shift: bfloat16 [768], P('shard'), may hold values from -1.75 to 1.75
- query_weight: bfloat16 [768, 768], P('shard'), may hold values from -0.21875 to 0.21875
- query_bias: bfloat16 [768], P('shard'), may hold values from -1.75 to 1.75
- key_weight: bfloat16 [768, 768], P('shard'), may hold values from -0.21875 to 0.21875
- value_weight: bfloat16 [768, 768], P('shard'), may hold values from -0.21875 to 0.21875
- value_bias: bfloat16 [768], P('shard'), may hold values from -1.75 to 1.75
- output_weight: bfloat16 [768, 768], P('shard'), may hold values from -0.4375 to 0.4375
- output_bias: bfloat16 [768], P('shard'), may hold values from -1.75 to 1.75
- second_gain: bfloat16 [768], P('shard'), may hold values from 0.5 to 1.5
- second_shift: bfloat16 [768], P('shard'), may hold values from -1.75 to 1.75
- inner_weight: bfloat16 [768, 3072], P('shard'), may hold values from -0.21875 to 0.21875
- inner_bias: bfloat16 [3072], P('shard'), may hold values from -1.75 to 1.75
- outer_weight: bfloat16 [3072, 768], P('shard'), may hold values from -0.109375 to 0.109375
- outer_bias: bfloat16 [768], P('shard'), may hold values from -1.75 to 1.75
Outputs:
- result: bfloat16 [32, 256, 768], P(('shard', 'rep'))
- input_grad: bfloat16 [32, 256, 768], P(('shard', 'rep'))
- grad_first_gain: float32 [768], P('shard')
- grad_first_shift: float32 [768], P('shard')
- grad_query_weight: float32 [768, 768], P('shard')
- grad_query_bias: float32 [768], P('shard')
- grad_key_weight: float32 [768, 768], P('shard')
- grad_value_weight: float32 [768, 768], P('shard')
- grad_value_bias: float32 [768], P('shard')
- grad_output_weight: float32 [768, 768], P('shard')
- grad_output_bias: float32 [768], P('shard')
- grad_second_gain: float32 [768], P('shard')
- grad_second_shift: float32 [768], P('shard')
- grad_inner_weight: float32 [768, 3072], P('shard')
- grad_inner_bias: float32 [3072], P('shard')
- grad_outer_weight: float32 [3072, 768], P('shard')
- grad_outer_bias: float32 [768], P('shard')
All inputs are finite; a program needn't handle non-finite values.
Results may differ from a plain program's by a relative error of at most 0.019.
Values may be sent and summed in bfloat16 or wider, within the bound.
A program may use at most 128 MiB of HBM per device.

v0:
```python
import jax
import jax.numpy as jnp
from jax import lax
from jax.sharding import PartitionSpec as P

D = 768
HEADS = 12
HD = 64


EPSILON = 1e-05


def normalize(values, gain, shift):
    center = jnp.mean(values, axis=-1, keepdims=True)
    spread = jnp.mean((values - center) ** 2, axis=-1, keepdims=True)
    inv_std = lax.rsqrt(spread + EPSILON)
    normed = (values - center) * inv_std
    return (normed * gain.astype(jnp.float32) + shift.astype(jnp.float32), normed, inv_std)


def norm_back(grad_out, normed, inv_std, gain):
    scaled = grad_out * gain.astype(jnp.float32)
    return inv_std * (
        scaled
        - jnp.mean(scaled, axis=-1, keepdims=True)
        - normed * jnp.mean(scaled * normed, axis=-1, keepdims=True)
    )


def gelu_parts(inner):
    cdf = 0.5 * (1.0 + jax.scipy.special.erf(inner * 0.7071067811865476))
    density = jnp.exp(-0.5 * inner * inner) * 0.3989422804014327
    return (inner * cdf, cdf + inner * density)


def heads_of(matrix):
    return matrix.reshape(matrix.shape[0], HEADS, HD)


def matmul(left, right):
    return jnp.dot(left, right, preferred_element_type=jnp.float32)


def forward_clip(clip, params):
    (
        first_gain,
        first_shift,
        query_weight,
        query_bias,
        key_weight,
        value_weight,
        value_bias,
        output_weight,
        output_bias,
        second_gain,
        second_shift,
        inner_weight,
        inner_bias,
        outer_weight,
        outer_bias,
    ) = params
    start = clip.astype(jnp.float32)
    normed_one, hat_one, inv_one = normalize(start, first_gain, first_shift)
    first_low = normed_one.astype(jnp.bfloat16)
    query = (
        (matmul(first_low, query_weight) + query_bias.astype(jnp.float32)) * HD ** (-0.5)
    ).astype(jnp.bfloat16)
    keys = matmul(first_low, key_weight).astype(jnp.bfloat16)
    values = (matmul(first_low, value_weight) + value_bias.astype(jnp.float32)).astype(jnp.bfloat16)
    scores = jnp.einsum(
        "qhd,khd->hqk", heads_of(query), heads_of(keys), preferred_element_type=jnp.float32
    )
    highest = jnp.max(scores, axis=-1, keepdims=True)
    log_total = highest + jnp.log(jnp.sum(jnp.exp(scores - highest), axis=-1, keepdims=True))
    probs = jnp.exp(scores - log_total).astype(jnp.bfloat16)
    context = (
        jnp.einsum("hqk,khd->qhd", probs, heads_of(values), preferred_element_type=jnp.float32)
        .reshape(-1, D)
        .astype(jnp.bfloat16)
    )
    mixed = start + matmul(context, output_weight) + output_bias.astype(jnp.float32)
    normed_two, hat_two, inv_two = normalize(mixed, second_gain, second_shift)
    second_low = normed_two.astype(jnp.bfloat16)
    inner = matmul(second_low, inner_weight) + inner_bias.astype(jnp.float32)
    active, slope = gelu_parts(inner)
    active_low = active.astype(jnp.bfloat16)
    result = (mixed + matmul(active_low, outer_weight) + outer_bias.astype(jnp.float32)).astype(
        jnp.bfloat16
    )
    saved = (
        hat_one,
        inv_one,
        first_low,
        query,
        keys,
        values,
        log_total,
        context,
        hat_two,
        inv_two,
        second_low,
        slope,
        active_low,
    )
    return (result, saved)


def backward_clip(grad_low, saved, params):
    (
        first_gain,
        first_shift,
        query_weight,
        query_bias,
        key_weight,
        value_weight,
        value_bias,
        output_weight,
        output_bias,
        second_gain,
        second_shift,
        inner_weight,
        inner_bias,
        outer_weight,
        outer_bias,
    ) = params
    (
        hat_one,
        inv_one,
        first_low,
        query,
        keys,
        values,
        log_total,
        context,
        hat_two,
        inv_two,
        second_low,
        slope,
        active_low,
    ) = saved
    grad = grad_low.astype(jnp.float32)
    g_outer_bias = jnp.sum(grad, axis=0)
    g_outer = matmul(active_low.T, grad_low)
    d_inner = matmul(grad_low, outer_weight.T) * slope
    d_inner_low = d_inner.astype(jnp.bfloat16)
    g_inner_bias = jnp.sum(d_inner, axis=0)
    g_inner = matmul(second_low.T, d_inner_low)
    d_second = matmul(d_inner_low, inner_weight.T)
    g_second_gain = jnp.sum(d_second * hat_two, axis=0)
    g_second_shift = jnp.sum(d_second, axis=0)
    d_mixed = grad + norm_back(d_second, hat_two, inv_two, second_gain)
    d_mixed_low = d_mixed.astype(jnp.bfloat16)
    g_output_bias = jnp.sum(d_mixed, axis=0)
    g_output = matmul(context.T, d_mixed_low)
    d_context = matmul(d_mixed_low, output_weight.T).astype(jnp.bfloat16)
    query_heads = heads_of(query)
    keys_heads = heads_of(keys)
    values_heads = heads_of(values)
    dctx_heads = heads_of(d_context)
    scores = jnp.einsum("qhd,khd->hqk", query_heads, keys_heads, preferred_element_type=jnp.float32)
    probs = jnp.exp(scores - log_total)
    probs_low = probs.astype(jnp.bfloat16)
    d_probs = jnp.einsum(
        "qhd,khd->hqk", dctx_heads, values_heads, preferred_element_type=jnp.float32
    )
    delta = jnp.sum(dctx_heads.astype(jnp.float32) * heads_of(context).astype(jnp.float32), axis=-1)
    d_scores = (probs * (d_probs - jnp.transpose(delta)[:, :, None])).astype(jnp.bfloat16)
    d_values = jnp.einsum(
        "hqk,qhd->khd", probs_low, dctx_heads, preferred_element_type=jnp.float32
    ).reshape(-1, D)
    d_query = jnp.einsum(
        "hqk,khd->qhd", d_scores, keys_heads, preferred_element_type=jnp.float32
    ).reshape(-1, D) * HD ** (-0.5)
    d_keys = jnp.einsum(
        "hqk,qhd->khd", d_scores, query_heads, preferred_element_type=jnp.float32
    ).reshape(-1, D)
    dq_low = d_query.astype(jnp.bfloat16)
    dk_low = d_keys.astype(jnp.bfloat16)
    dv_low = d_values.astype(jnp.bfloat16)
    g_query_bias = jnp.sum(d_query, axis=0)
    g_value_bias = jnp.sum(d_values, axis=0)
    g_query = matmul(first_low.T, dq_low)
    g_keys = matmul(first_low.T, dk_low)
    g_values = matmul(first_low.T, dv_low)
    d_first = (
        matmul(dq_low, query_weight.T)
        + matmul(dk_low, key_weight.T)
        + matmul(dv_low, value_weight.T)
    )
    g_first_gain = jnp.sum(d_first * hat_one, axis=0)
    g_first_shift = jnp.sum(d_first, axis=0)
    d_start = (d_mixed + norm_back(d_first, hat_one, inv_one, first_gain)).astype(jnp.bfloat16)
    grads = (
        g_first_gain,
        g_first_shift,
        g_query,
        g_query_bias,
        g_keys,
        g_values,
        g_value_bias,
        g_output,
        g_output_bias,
        g_second_gain,
        g_second_shift,
        g_inner,
        g_inner_bias,
        g_outer,
        g_outer_bias,
    )
    return (d_start, grads)


def per_device(
    frames,
    cotangent,
    first_gain,
    first_shift,
    query_weight,
    query_bias,
    key_weight,
    value_weight,
    value_bias,
    output_weight,
    output_bias,
    second_gain,
    second_shift,
    inner_weight,
    inner_bias,
    outer_weight,
    outer_bias,
):
    params = (
        lax.all_gather(first_gain, "shard", axis=0, tiled=True),
        lax.all_gather(first_shift, "shard", axis=0, tiled=True),
        lax.all_gather(query_weight, "shard", axis=0, tiled=True),
        lax.all_gather(query_bias, "shard", axis=0, tiled=True),
        lax.all_gather(key_weight, "shard", axis=0, tiled=True),
        lax.all_gather(value_weight, "shard", axis=0, tiled=True),
        lax.all_gather(value_bias, "shard", axis=0, tiled=True),
        lax.all_gather(output_weight, "shard", axis=0, tiled=True),
        lax.all_gather(output_bias, "shard", axis=0, tiled=True),
        lax.all_gather(second_gain, "shard", axis=0, tiled=True),
        lax.all_gather(second_shift, "shard", axis=0, tiled=True),
        lax.all_gather(inner_weight, "shard", axis=0, tiled=True),
        lax.all_gather(inner_bias, "shard", axis=0, tiled=True),
        lax.all_gather(outer_weight, "shard", axis=0, tiled=True),
        lax.all_gather(outer_bias, "shard", axis=0, tiled=True),
    )

    def forward_step(carry, clip):
        result, saved = forward_clip(clip, params)
        return (carry, (result, saved))

    unused, (results, stored) = lax.scan(forward_step, jnp.zeros((), jnp.float32), frames)

    def backward_step(totals, pair):
        grad_low, saved = pair
        d_start, grads = backward_clip(grad_low, saved, params)
        return (tuple((total + piece for total, piece in zip(totals, grads))), d_start)

    zeros = tuple((jnp.zeros(weight.shape, jnp.float32) for weight in params))
    totals, input_grad = lax.scan(backward_step, zeros, (cotangent, stored))
    shares = (
        lax.psum_scatter(
            totals[0].astype(jnp.bfloat16), "shard", scatter_dimension=0, tiled=True
        ).astype(jnp.float32),
        lax.psum_scatter(
            totals[1].astype(jnp.bfloat16), "shard", scatter_dimension=0, tiled=True
        ).astype(jnp.float32),
        lax.psum_scatter(
            totals[2].astype(jnp.bfloat16), "shard", scatter_dimension=0, tiled=True
        ).astype(jnp.float32),
        lax.psum_scatter(
            totals[3].astype(jnp.bfloat16), "shard", scatter_dimension=0, tiled=True
        ).astype(jnp.float32),
        lax.psum_scatter(
            totals[4].astype(jnp.bfloat16), "shard", scatter_dimension=0, tiled=True
        ).astype(jnp.float32),
        lax.psum_scatter(
            totals[5].astype(jnp.bfloat16), "shard", scatter_dimension=0, tiled=True
        ).astype(jnp.float32),
        lax.psum_scatter(
            totals[6].astype(jnp.bfloat16), "shard", scatter_dimension=0, tiled=True
        ).astype(jnp.float32),
        lax.psum_scatter(
            totals[7].astype(jnp.bfloat16), "shard", scatter_dimension=0, tiled=True
        ).astype(jnp.float32),
        lax.psum_scatter(
            totals[8].astype(jnp.bfloat16), "shard", scatter_dimension=0, tiled=True
        ).astype(jnp.float32),
        lax.psum_scatter(
            totals[9].astype(jnp.bfloat16), "shard", scatter_dimension=0, tiled=True
        ).astype(jnp.float32),
        lax.psum_scatter(
            totals[10].astype(jnp.bfloat16), "shard", scatter_dimension=0, tiled=True
        ).astype(jnp.float32),
        lax.psum_scatter(
            totals[11].astype(jnp.bfloat16), "shard", scatter_dimension=0, tiled=True
        ).astype(jnp.float32),
        lax.psum_scatter(
            totals[12].astype(jnp.bfloat16), "shard", scatter_dimension=0, tiled=True
        ).astype(jnp.float32),
        lax.psum_scatter(
            totals[13].astype(jnp.bfloat16), "shard", scatter_dimension=0, tiled=True
        ).astype(jnp.float32),
        lax.psum_scatter(
            totals[14].astype(jnp.bfloat16), "shard", scatter_dimension=0, tiled=True
        ).astype(jnp.float32),
    )
    summed = (
        lax.psum(shares[0].astype(jnp.bfloat16), "rep").astype(jnp.float32),
        lax.psum(shares[1].astype(jnp.bfloat16), "rep").astype(jnp.float32),
        lax.psum(shares[2].astype(jnp.bfloat16), "rep").astype(jnp.float32),
        lax.psum(shares[3].astype(jnp.bfloat16), "rep").astype(jnp.float32),
        lax.psum(shares[4].astype(jnp.bfloat16), "rep").astype(jnp.float32),
        lax.psum(shares[5].astype(jnp.bfloat16), "rep").astype(jnp.float32),
        lax.psum(shares[6].astype(jnp.bfloat16), "rep").astype(jnp.float32),
        lax.psum(shares[7].astype(jnp.bfloat16), "rep").astype(jnp.float32),
        lax.psum(shares[8].astype(jnp.bfloat16), "rep").astype(jnp.float32),
        lax.psum(shares[9].astype(jnp.bfloat16), "rep").astype(jnp.float32),
        lax.psum(shares[10].astype(jnp.bfloat16), "rep").astype(jnp.float32),
        lax.psum(shares[11].astype(jnp.bfloat16), "rep").astype(jnp.float32),
        lax.psum(shares[12].astype(jnp.bfloat16), "rep").astype(jnp.float32),
        lax.psum(shares[13].astype(jnp.bfloat16), "rep").astype(jnp.float32),
        lax.psum(shares[14].astype(jnp.bfloat16), "rep").astype(jnp.float32),
    )
    return (
        results,
        input_grad,
        summed[0],
        summed[1],
        summed[2],
        summed[3],
        summed[4],
        summed[5],
        summed[6],
        summed[7],
        summed[8],
        summed[9],
        summed[10],
        summed[11],
        summed[12],
        summed[13],
        summed[14],
    )


def solution(mesh):
    placed = (
        P(("shard", "rep"), None, None),
        P(("shard", "rep"), None, None),
        P("shard"),
        P("shard"),
        P("shard", None),
        P("shard"),
        P("shard", None),
        P("shard", None),
        P("shard"),
        P("shard", None),
        P("shard"),
        P("shard"),
        P("shard"),
        P("shard", None),
        P("shard"),
        P("shard", None),
        P("shard"),
    )
    return jax.shard_map(
        per_device,
        mesh=mesh,
        in_specs=placed,
        out_specs=(
            P(("shard", "rep"), None, None),
            P(("shard", "rep"), None, None),
            P("shard"),
            P("shard"),
            P("shard", None),
            P("shard"),
            P("shard", None),
            P("shard", None),
            P("shard"),
            P("shard", None),
            P("shard"),
            P("shard"),
            P("shard"),
            P("shard", None),
            P("shard"),
            P("shard", None),
            P("shard"),
        ),
        check_vma=False,
    )
```

profile of v0, /device:TPU:0, one launch (start us, length us, event | category | flops | bytes accessed | tf_op | source)
XLA Modules:
  0.0 805.8 jit_solution(6576003096253520976)
XLA Ops:
  20.6 63.2 %all-reduce.19 = (bf16[768]{0:T(1024)(128)(2,1)S(1)}, bf16[768]{0:T(1024)(128)(2,1)S(1)}, bf16[768]{0:T(1024)(128)(2,1)S(1)}, bf16[768]{0:T(1024)(128)(2,1)S(1)}...) all-reduce(bf16[768]{0:T(1024)(128)(2,1)S(1)} %dynamic-update-slice, ...), channel_id=1, replica_groups=mesh['shard'=16,'rep'=2] {'shard'}, use_global_device_ids=true, to_apply=%add.2 | all-reduce | flops 8448 | bytes 33792
  88.7 2.0 fusion.9
  91.6 1.8 fusion.10
  94.3 36.1 %all-gather.11.cloned.1.call-done = bf16[768,768]{1,0:T(8,128)(2,1)} async-done(((bf16[48,768]{1,0:T(8,128)(2,1)}), bf16[768,768]{1,0:T(8,128)(2,1)}) %all-gather.11.cloned.1.call-update) | async-done | bytes 1179664 | tf_op jit(solution)/shard_map/all_gather | solution.py:238
  136.8 32.9 %all-gather.13.cloned.1.call-done = bf16[768,768]{1,0:T(8,128)(2,1)} async-done(((bf16[48,768]{1,0:T(8,128)(2,1)}), bf16[768,768]{1,0:T(8,128)(2,1)}) %all-gather.13.cloned.1.call-update) | async-done | bytes 1179664 | tf_op jit(solution)/shard_map/all_gather | solution.py:241
  169.7 1.9 fusion.53
  173.4 50.5 %all-gather.15.cloned.1.call-done = bf16[768,3072]{1,0:T(8,128)(2,1)} async-done(((bf16[48,3072]{1,0:T(8,128)(2,1)}), bf16[768,3072]{1,0:T(8,128)(2,1)}) %all-gather.15.cloned.1.call-update) | async-done | bytes 4718608 | tf_op jit(solution)/shard_map/all_gather | solution.py:245
  223.9 6.5 multiply_convert_fusion.1
  230.4 47.3 %all-gather.17.cloned.1.call-done = bf16[3072,768]{1,0:T(8,128)(2,1)} async-done(((bf16[192,768]{1,0:T(8,128)(2,1)}), bf16[3072,768]{1,0:T(8,128)(2,1)}) %all-gather.17.cloned.1.call-update) | async-done | bytes 4718608 | tf_op jit(solution)/shard_map/all_gather | solution.py:247
  277.8 6.0 fusion.54
  283.8 2.2 multiply_reduce_fusion
  289.1 1.9 copy.59
  292.4 1.9 multiply_convert_fusion
  298.9 2.1 convolution_convert_fusion.6
  301.8 2.4 convolution_convert_fusion.4
  304.3 2.3 fusion.50
  310.9 5.2 convolution_convert_fusion.1
  317.1 5.1 convolution_convert_fusion
  324.5 1.9 fusion.55
  327.1 3.3 fusion.26
  331.5 24.1 %reduce-scatter.7.cloned.1.call-done = bf16[48,768]{1,0:T(8,128)(2,1)} async-done(((bf16[768,768]{1,0:T(8,128)(2,1)}), bf16[48,768]{1,0:T(8,128)(2,1)}) %reduce-scatter.7.cloned.1.call-update) | async-done | bytes 73744 | tf_op jit(solution)/shard_map/reduce_scatter | solution.py:271
  355.6 60.8 %reduce-scatter.9.cloned.1.call-done = bf16[48,768]{1,0:T(8,128)(2,1)} async-done(((bf16[768,768]{1,0:T(8,128)(2,1)}), bf16[48,768]{1,0:T(8,128)(2,1)}) %reduce-scatter.9.cloned.1.call-update) | async-done | bytes 73744 | tf_op jit(solution)/shard_map/reduce_scatter | solution.py:277
  416.4 60.7 %reduce-scatter.11.cloned.1.call-done = bf16[48,768]{1,0:T(8,128)(2,1)} async-done(((bf16[768,768]{1,0:T(8,128)(2,1)}), bf16[48,768]{1,0:T(8,128)(2,1)}) %reduce-scatter.11.cloned.1.call-update) | async-done | bytes 73744 | tf_op jit(solution)/shard_map/reduce_scatter | solution.py:280
  477.1 60.7 %reduce-scatter.13.cloned.1.call-done = bf16[48,768]{1,0:T(8,128)(2,1)} async-done(((bf16[768,768]{1,0:T(8,128)(2,1)}), bf16[48,768]{1,0:T(8,128)(2,1)}) %reduce-scatter.13.cloned.1.call-update) | async-done | bytes 73744 | tf_op jit(solution)/shard_map/reduce_scatter | solution.py:286
  537.8 78.5 %reduce-scatter.15.cloned.1.call-done = bf16[48,3072]{1,0:T(8,128)(2,1)} async-done(((bf16[768,3072]{1,0:T(8,128)(2,1)}), bf16[48,3072]{1,0:T(8,128)(2,1)}) %reduce-scatter.15.cloned.1.call-update) | async-done | bytes 294928 | tf_op jit(solution)/shard_map/reduce_scatter | solution.py:298
  616.3 78.5 %reduce-scatter.17.cloned.1.call-done = bf16[192,768]{1,0:T(8,128)(2,1)} async-done(((bf16[3072,768]{1,0:T(8,128)(2,1)}), bf16[192,768]{1,0:T(8,128)(2,1)}) %reduce-scatter.17.cloned.1.call-update) | async-done | bytes 294928 | tf_op jit(solution)/shard_map/reduce_scatter | solution.py:304
  696.9 58.2 %all-reduce.18 = (bf16[768]{0:T(1024)(128)(2,1)}, bf16[768]{0:T(1024)(128)(2,1)}, bf16[768]{0:T(1024)(128)(2,1)}, bf16[768]{0:T(1024)(128)(2,1)}, bf16[768]{0:T(...) all-reduce(bf16[768]{0:T(1024)(128)(2,1)} %copy-done.37, ...), channel_id=1, replica_groups=mesh['shard'=16,'rep'=2] {'shard'}, use_global_device_ids=true, to_apply=%add.8 | all-reduce | flops 9984 | bytes 39936
  766.6 5.6 all-reduce.20
  782.8 2.2 fusion.38
  785.0 4.5 fusion.11
  795.7 1.8 convert_element_type.362
  797.5 1.8 convert_element_type.366
  (205 shorter events, 74.5 us)
Async XLA Ops:
  7.2 84.4 %copy-start.6 = (bf16[1,256,768]{2,1,0:T(8,128)(2,1)S(1)}, bf16[1,256,768]{2,1,0:T(8,128)(2,1)}, u32[]{:S(2)}) copy-start(bf16[1,256,768]{2,1,0:T(8,128)(2,1)} %param.17) | copy-start | bytes 1179652
  7.2 81.5 %all-gather.7.cloned.1.call-start = ((), (), s32[]{:S(2)}) async-start(), calls=%async_computation.6 | async-start | bytes 1253376 | tf_op jit(solution)/shard_map/all_gather | solution.py:239
  7.9 83.6 %all-gather.9.cloned.1.call-start = ((), (), s32[]{:S(2)}) async-start(), calls=%async_computation.7 | async-start | bytes 1253376 | tf_op jit(solution)/shard_map/all_gather | solution.py:236
  8.7 121.7 %all-gather.11.cloned.1.call-start = ((), (), s32[]{:S(2)}) async-start(), calls=%async_computation.8 | async-start | bytes 1253376 | tf_op jit(solution)/shard_map/all_gather | solution.py:238
  9.4 160.3 %all-gather.13.cloned.1.call-start = ((), (), s32[]{:S(2)}) async-start(), calls=%async_computation.9 | async-start | bytes 1253376 | tf_op jit(solution)/shard_map/all_gather | solution.py:241
  10.0 213.9 %all-gather.15.cloned.1.call-start = ((), (), s32[]{:S(2)}) async-start(), calls=%async_computation.10 | async-start | bytes 5013504 | tf_op jit(solution)/shard_map/all_gather | solution.py:245
  10.6 267.2 %all-gather.17.cloned.1.call-start = ((), (), s32[]{:S(2)}) async-start(), calls=%async_computation.11 | async-start | bytes 5013504 | tf_op jit(solution)/shard_map/all_gather | solution.py:247
  11.2 344.4 %reduce-scatter.7.cloned.1.call-start = ((), (), s32[]{:S(2)}) async-start(), calls=%async_computation.12 | async-start | bytes 1253376 | tf_op jit(solution)/shard_map/reduce_scatter | solution.py:271
  84.4 46.0 %copy-start.42 = (f32[768]{0:T(1024)}, f32[768]{0:T(1024)S(1)}, u32[]{:S(2)}) copy-start(f32[768]{0:T(1024)S(1)} %convert_element_type.298) | copy-start | bytes 9220
  84.4 46.0 %copy-start.26 = (f32[768]{0:T(1024)}, f32[768]{0:T(1024)S(1)}, u32[]{:S(2)}) copy-start(f32[768]{0:T(1024)S(1)} %convert_element_type.297) | copy-start | bytes 9220
  87.4 43.0 %copy-start.33 = (f32[256]{0:T(256)}, f32[256]{0:T(256)S(1)}, u32[]{:S(2)}) copy-start(f32[256]{0:T(256)S(1)} %broadcast_multiply_fusion.5) | copy-start | bytes 3076
  88.6 41.8 %copy-start.38 = (f32[256]{0:T(256)}, f32[256]{0:T(256)S(1)}, u32[]{:S(2)}) copy-start(f32[256]{0:T(256)S(1)} %add_rsqrt_fusion.1) | copy-start | bytes 3076
  277.7 6.0 copy-start.1
  277.7 6.0 copy-start.20
  277.8 6.0 copy-start.24
  277.8 6.0 copy-start.31
  277.8 6.1 copy-start.45
  291.1 4.4 copy-start.12
  298.7 117.7 %reduce-scatter.9.cloned.1.call-start = ((), (), s32[]{:S(2)}) async-start(), calls=%async_computation.13 | async-start | bytes 1253376 | tf_op jit(solution)/shard_map/reduce_scatter | solution.py:277
  304.3 172.8 %reduce-scatter.11.cloned.1.call-start = ((), (), s32[]{:S(2)}) async-start(), calls=%async_computation.14 | async-start | bytes 1253376 | tf_op jit(solution)/shard_map/reduce_scatter | solution.py:280
  307.4 3.4 copy-start.2
  307.4 3.4 copy-start.21
  309.2 228.6 %reduce-scatter.13.cloned.1.call-start = ((), (), s32[]{:S(2)}) async-start(), calls=%async_computation.15 | async-start | bytes 1253376 | tf_op jit(solution)/shard_map/reduce_scatter | solution.py:286
  310.8 305.5 %reduce-scatter.15.cloned.1.call-start = ((), (), s32[]{:S(2)}) async-start(), calls=%async_computation.16 | async-start | bytes 5013504 | tf_op jit(solution)/shard_map/reduce_scatter | solution.py:298
  316.2 378.7 %reduce-scatter.17.cloned.1.call-start = ((), (), s32[]{:S(2)}) async-start(), calls=%async_computation.17 | async-start | bytes 5013504 | tf_op jit(solution)/shard_map/reduce_scatter | solution.py:304
  322.2 4.3 copy-start.16
  322.2 4.8 copy-start.29
  322.2 4.8 copy-start.36
  322.2 4.8 copy-start.41
  322.3 467.2 %all-reduce.24.cloned.1.call-start = ((), (), s32[]{:S(2)}) async-start(), calls=%async_computation.18 | async-start | bytes 1769472 | tf_op jit(solution)/shard_map/psum | solution.py:314
  327.1 369.7 %copy-start.30 = (bf16[12,64]{1,0:T(8,128)(2,1)S(1)}, bf16[12,64]{1,0:T(8,128)(2,1)}, u32[]{:S(2)}) copy-start(bf16[12,64]{1,0:T(8,128)(2,1)} %get-tuple-element.233) | copy-start | bytes 4612
  327.1 457.9 %copy-start.11 = (bf16[256,3072]{1,0:T(8,128)(2,1)S(1)}, bf16[256,3072]{1,0:T(8,128)(2,1)}, u32[]{:S(2)}) copy-start(bf16[256,3072]{1,0:T(8,128)(2,1)} %get-tuple-element.280) | copy-start | bytes 4718596
  (29 other events, 59.8 us)
Sparse Core Ops, SparseCore 0:
  10.3 41.0 all-gather.6
  53.7 37.1 all-gather.8
  93.2 37.1 all-gather.10
  132.5 37.1 all-gather.12
  171.9 51.9 all-gather.14
  226.0 51.6 all-gather.16
  298.8 56.7 reduce-scatter.6
  359.2 57.1 reduce-scatter.8
  420.0 57.0 reduce-scatter.10
  480.6 57.1 reduce-scatter.12
  541.6 74.6 reduce-scatter.14
  620.0 74.7 reduce-scatter.16
  697.5 35.7 all-reduce.23
where the time goes:
time: 807 us; the launch traced here: 806 us
  waiting for transfers between devices  534 us (66%)
  blocking collectives  127 us (16%)
  matrix products  62.3 us (8%)
  other arithmetic  34.6 us (4%)
  local copies, waits for them, and re-layouts  30.1 us (4%)
  between operations  17.1 us (2%)
    unnamed x2, blocking collectives  121 us
    reduce_scatter x1, waiting for transfers between devices, per_device(): lax.psum_scatter(totals[11].astype(jnp.bfloat16), 'shard', scatter_dimens...  78.5 us
    reduce_scatter x1, waiting for transfers between devices, per_device(): lax.psum_scatter(totals[13].astype(jnp.bfloat16), 'shard', scatter_dimens...  78.5 us
    reduce_scatter x1, waiting for transfers between devices, per_device(): lax.psum_scatter(totals[4].astype(jnp.bfloat16), 'shard', scatter_dimensi...  60.8 us
    reduce_scatter x1, waiting for transfers between devices, per_device(): lax.psum_scatter(totals[5].astype(jnp.bfloat16), 'shard', scatter_dimensi...  60.7 us
    reduce_scatter x1, waiting for transfers between devices, per_device(): lax.psum_scatter(totals[7].astype(jnp.bfloat16), 'shard', scatter_dimensi...  60.7 us
    dot_general x18, matrix products, matmul(): return jnp.dot(left, right, preferred_element_type=jnp.float32)  51.4 us
    all_gather x1, waiting for transfers between devices, per_device(): lax.all_gather(inner_weight, 'shard', axis=0, tiled=True)  50.5 us
  transfers between devices with their start and end apart: 13, of which 10 were waited for; matrix products, arithmetic and copies ran while one was open for 12% of the time, Pallas kernels for 0%

commit v1 on v0

v1 whole, which is shorter than its diff:
```python
import functools

import jax
import jax.numpy as jnp
from jax import lax
from jax.experimental import pallas as pl
from jax.experimental.pallas import tpu as pltpu
from jax.sharding import PartitionSpec as P

D = 768
HEADS = 12
HD = 64


EPSILON = 1e-05


def normalize(values, gain, shift):
    center = jnp.mean(values, axis=-1, keepdims=True)
    spread = jnp.mean((values - center) ** 2, axis=-1, keepdims=True)
    inv_std = lax.rsqrt(spread + EPSILON)
    normed = (values - center) * inv_std
    return (normed * gain.astype(jnp.float32) + shift.astype(jnp.float32), normed, inv_std)


def norm_back(grad_out, normed, inv_std, gain):
    scaled = grad_out * gain.astype(jnp.float32)
    return inv_std * (
        scaled
        - jnp.mean(scaled, axis=-1, keepdims=True)
        - normed * jnp.mean(scaled * normed, axis=-1, keepdims=True)
    )


def gelu_parts(inner):
    cdf = 0.5 * (1.0 + jax.scipy.special.erf(inner * 0.7071067811865476))
    density = jnp.exp(-0.5 * inner * inner) * 0.3989422804014327
    return (inner * cdf, cdf + inner * density)


def heads_of(matrix):
    return matrix.reshape(matrix.shape[0], HEADS, HD)


def matmul(left, right):
    return jnp.dot(left, right, preferred_element_type=jnp.float32)


def forward_clip(clip, params):
    (
        first_gain,
        first_shift,
        query_weight,
        query_bias,
        key_weight,
        value_weight,
        value_bias,
        output_weight,
        output_bias,
        second_gain,
        second_shift,
        inner_weight,
        inner_bias,
        outer_weight,
        outer_bias,
    ) = params
    start = clip.astype(jnp.float32)
    normed_one, hat_one, inv_one = normalize(start, first_gain, first_shift)
    first_low = normed_one.astype(jnp.bfloat16)
    query = (
        (matmul(first_low, query_weight) + query_bias.astype(jnp.float32)) * HD ** (-0.5)
    ).astype(jnp.bfloat16)
    keys = matmul(first_low, key_weight).astype(jnp.bfloat16)
    values = (matmul(first_low, value_weight) + value_bias.astype(jnp.float32)).astype(jnp.bfloat16)
    scores = jnp.einsum(
        "qhd,khd->hqk", heads_of(query), heads_of(keys), preferred_element_type=jnp.float32
    )
    highest = jnp.max(scores, axis=-1, keepdims=True)
    log_total = highest + jnp.log(jnp.sum(jnp.exp(scores - highest), axis=-1, keepdims=True))
    probs = jnp.exp(scores - log_total).astype(jnp.bfloat16)
    context = (
        jnp.einsum("hqk,khd->qhd", probs, heads_of(values), preferred_element_type=jnp.float32)
        .reshape(-1, D)
        .astype(jnp.bfloat16)
    )
    mixed = start + matmul(context, output_weight) + output_bias.astype(jnp.float32)
    normed_two, hat_two, inv_two = normalize(mixed, second_gain, second_shift)
    second_low = normed_two.astype(jnp.bfloat16)
    inner = matmul(second_low, inner_weight) + inner_bias.astype(jnp.float32)
    active, slope = gelu_parts(inner)
    active_low = active.astype(jnp.bfloat16)
    result = (mixed + matmul(active_low, outer_weight) + outer_bias.astype(jnp.float32)).astype(
        jnp.bfloat16
    )
    saved = (
        hat_one,
        inv_one,
        first_low,
        query,
        keys,
        values,
        log_total,
        context,
        hat_two,
        inv_two,
        second_low,
        slope,
        active_low,
    )
    return (result, saved)


def backward_clip(grad_low, saved, params):
    (
        first_gain,
        first_shift,
        query_weight,
        query_bias,
        key_weight,
        value_weight,
        value_bias,
        output_weight,
        output_bias,
        second_gain,
        second_shift,
        inner_weight,
        inner_bias,
        outer_weight,
        outer_bias,
    ) = params
    (
        hat_one,
        inv_one,
        first_low,
        query,
        keys,
        values,
        log_total,
        context,
        hat_two,
        inv_two,
        second_low,
        slope,
        active_low,
    ) = saved
    grad = grad_low.astype(jnp.float32)
    g_outer_bias = jnp.sum(grad, axis=0)
    g_outer = matmul(active_low.T, grad_low)
    d_inner = matmul(grad_low, outer_weight.T) * slope
    d_inner_low = d_inner.astype(jnp.bfloat16)
    g_inner_bias = jnp.sum(d_inner, axis=0)
    g_inner = matmul(second_low.T, d_inner_low)
    d_second = matmul(d_inner_low, inner_weight.T)
    g_second_gain = jnp.sum(d_second * hat_two, axis=0)
    g_second_shift = jnp.sum(d_second, axis=0)
    d_mixed = grad + norm_back(d_second, hat_two, inv_two, second_gain)
    d_mixed_low = d_mixed.astype(jnp.bfloat16)
    g_output_bias = jnp.sum(d_mixed, axis=0)
    g_output = matmul(context.T, d_mixed_low)
    d_context = matmul(d_mixed_low, output_weight.T).astype(jnp.bfloat16)
    query_heads = heads_of(query)
    keys_heads = heads_of(keys)
    values_heads = heads_of(values)
    dctx_heads = heads_of(d_context)
    scores = jnp.einsum("qhd,khd->hqk", query_heads, keys_heads, preferred_element_type=jnp.float32)
    probs = jnp.exp(scores - log_total)
    probs_low = probs.astype(jnp.bfloat16)
    d_probs = jnp.einsum(
        "qhd,khd->hqk", dctx_heads, values_heads, preferred_element_type=jnp.float32
    )
    delta = jnp.sum(dctx_heads.astype(jnp.float32) * heads_of(context).astype(jnp.float32), axis=-1)
    d_scores = (probs * (d_probs - jnp.transpose(delta)[:, :, None])).astype(jnp.bfloat16)
    d_values = jnp.einsum(
        "hqk,qhd->khd", probs_low, dctx_heads, preferred_element_type=jnp.float32
    ).reshape(-1, D)
    d_query = jnp.einsum(
        "hqk,khd->qhd", d_scores, keys_heads, preferred_element_type=jnp.float32
    ).reshape(-1, D) * HD ** (-0.5)
    d_keys = jnp.einsum(
        "hqk,qhd->khd", d_scores, query_heads, preferred_element_type=jnp.float32
    ).reshape(-1, D)
    dq_low = d_query.astype(jnp.bfloat16)
    dk_low = d_keys.astype(jnp.bfloat16)
    dv_low = d_values.astype(jnp.bfloat16)
    g_query_bias = jnp.sum(d_query, axis=0)
    g_value_bias = jnp.sum(d_values, axis=0)
    g_query = matmul(first_low.T, dq_low)
    g_keys = matmul(first_low.T, dk_low)
    g_values = matmul(first_low.T, dv_low)
    d_first = (
        matmul(dq_low, query_weight.T)
        + matmul(dk_low, key_weight.T)
        + matmul(dv_low, value_weight.T)
    )
    g_first_gain = jnp.sum(d_first * hat_one, axis=0)
    g_first_shift = jnp.sum(d_first, axis=0)
    d_start = (d_mixed + norm_back(d_first, hat_one, inv_one, first_gain)).astype(jnp.bfloat16)
    grads = (
        g_first_gain,
        g_first_shift,
        g_query,
        g_query_bias,
        g_keys,
        g_values,
        g_value_bias,
        g_output,
        g_output_bias,
        g_second_gain,
        g_second_shift,
        g_inner,
        g_inner_bias,
        g_outer,
        g_outer_bias,
    )
    return (d_start, grads)


MESH = pl.DeviceIdType.MESH


class Ring:
    def __init__(self, chips):
        self.chips = chips
        shard = lax.axis_index("shard")
        self.rep = lax.axis_index("rep")
        self.core = lax.rem(shard, 2)
        chip = shard // 2
        half = chip // 2
        self.pos = half + lax.rem(chip, 2) * (chips - 1 - 2 * half)
        self.step = 1 - 2 * self.core
        self.me = shard
        self.mate = chip * 2 + (1 - self.core)

    def shard_at(self, offset, core):
        place = lax.rem(self.pos + offset + 2 * self.chips, self.chips)
        far = place // (self.chips // 2)
        chip = (1 - far) * 2 * place + far * (2 * (self.chips - 1 - place) + 1)
        return chip * 2 + core

    def next(self):
        return self.shard_at(self.step, self.core)

    def previous(self):
        return self.shard_at(-self.step, self.core)


def rows_of(owner, rows):
    return pl.ds(pl.multiple_of(owner * rows, rows), rows)


def greet(ring, others, reps):
    barrier = pltpu.get_barrier_semaphore()
    for other in others:
        pl.semaphore_signal(barrier, inc=1, device_id=(other, ring.rep), device_id_type=MESH)
    for shift in range(1, reps):
        pl.semaphore_signal(
            barrier,
            inc=1,
            device_id=(ring.me, lax.rem(ring.rep + shift, reps)),
            device_id_type=MESH,
        )
    pl.semaphore_wait(barrier, len(others) + reps - 1)


def gather_kernel(chips, count, *refs):
    ins, outs = refs[:count], refs[count : 2 * count]
    ring_send, ring_recv, mate_send, mate_recv, own_sem = refs[2 * count :]
    ring = Ring(chips)
    core = ring.core
    following, mate = ring.next(), ring.mate
    greet(ring, (following, ring.previous(), mate), 1)

    def where(index, owner):
        return outs[index].at[rows_of(owner, ins[index].shape[0])]

    def to_next(index, step, owner, source):
        return pltpu.make_async_remote_copy(
            src_ref=source,
            dst_ref=where(index, owner),
            send_sem=ring_send.at[step, index],
            recv_sem=ring_recv.at[step, index],
            device_id=(following, ring.rep),
            device_id_type=MESH,
        )

    def to_mate(index, step, owner, source):
        return pltpu.make_async_remote_copy(
            src_ref=source,
            dst_ref=where(index, owner),
            send_sem=mate_send.at[step, index],
            recv_sem=mate_recv.at[step, index],
            device_id=(mate, ring.rep),
            device_id_type=MESH,
        )

    for index in range(count):
        to_next(index, 0, ring.me, ins[index]).start()
    for index in range(count):
        to_mate(index, 0, ring.me, ins[index]).start()
        pltpu.make_async_copy(ins[index], where(index, ring.me), own_sem.at[index]).start()

    def hop(step, carry):
        owner = ring.shard_at(-ring.step * step, core)
        for index in range(count):
            block = where(index, owner)
            to_next(index, step - 1, owner, block).wait_recv()
            pl.when(step < chips - 1)(lambda: to_next(index, step, owner, block).start())
            to_mate(index, step, owner, block).start()
        return carry

    lax.fori_loop(1, chips, hop, 0)

    def finish(step, carry):
        owner = ring.shard_at(-ring.step * step, core)
        theirs = ring.shard_at(ring.step * step, 1 - core)
        for index in range(count):
            to_mate(index, step, theirs, where(index, theirs)).wait_recv()
            to_mate(index, step, owner, where(index, owner)).wait_send()
            pl.when(step < chips - 1)(
                lambda: to_next(index, step, owner, where(index, owner)).wait_send()
            )
        return carry

    lax.fori_loop(0, chips, finish, 0)
    for index in range(count):
        pltpu.make_async_copy(ins[index], where(index, ring.me), own_sem.at[index]).wait()


def gather_all(pieces, shards):
    chips, count = shards // 2, len(pieces)
    return pl.pallas_call(
        functools.partial(gather_kernel, chips, count),
        out_shape=[
            jax.ShapeDtypeStruct((piece.shape[0] * shards, piece.shape[1]), piece.dtype)
            for piece in pieces
        ],
        in_specs=[pl.BlockSpec(memory_space=pltpu.VMEM)] * count,
        out_specs=[pl.BlockSpec(memory_space=pl.ANY)] * count,
        scratch_shapes=[
            pltpu.SemaphoreType.DMA((chips, count)),
            pltpu.SemaphoreType.DMA((chips, count)),
            pltpu.SemaphoreType.DMA((chips, count)),
            pltpu.SemaphoreType.DMA((chips, count)),
            pltpu.SemaphoreType.DMA((count,)),
        ],
        compiler_params=pltpu.CompilerParams(collective_id=0, has_side_effects=True),
        name="gather_all",
    )(*pieces)


def scatter_kernel(chips, reps, count, *refs):
    ins, outs = refs[:count], refs[count : 2 * count]
    held = refs[2 * count : 3 * count]
    arrived = refs[3 * count : 4 * count]
    peers = refs[4 * count : 5 * count]
    ring_send, ring_recv, mate_send, mate_recv, rep_send, rep_recv = refs[5 * count :]
    ring = Ring(chips)
    core = ring.core
    following, mate = ring.next(), ring.mate
    greet(ring, (following, ring.previous(), mate), reps)

    def to_mate(index, step):
        owner = ring.shard_at(ring.step * (step + 1), 1 - core)
        rows = outs[index].shape[0]
        return pltpu.make_async_remote_copy(
            src_ref=ins[index].at[rows_of(owner, rows)],
            dst_ref=held[index].at[step],
            send_sem=mate_send.at[step, index],
            recv_sem=mate_recv.at[step, index],
            device_id=(mate, ring.rep),
            device_id_type=MESH,
        )

    def to_next(index, step):
        return pltpu.make_async_remote_copy(
            src_ref=held[index].at[step],
            dst_ref=arrived[index].at[step],
            send_sem=ring_send.at[step, index],
            recv_sem=ring_recv.at[step, index],
            device_id=(following, ring.rep),
            device_id_type=MESH,
        )

    def to_rep(index, shift):
        return pltpu.make_async_remote_copy(
            src_ref=held[index].at[chips - 1],
            dst_ref=peers[index].at[ring.rep],
            send_sem=rep_send.at[shift, index],
            recv_sem=rep_recv.at[shift, index],
            device_id=(ring.me, lax.rem(ring.rep + shift, reps)),
            device_id_type=MESH,
        )

    def hand_over(step, carry):
        for index in range(count):
            to_mate(index, step).start()
        return carry

    lax.fori_loop(0, chips, hand_over, 0)

    def add(index, step, first):
        owner = ring.shard_at(-ring.step * (step + 1), core)
        rows = outs[index].shape[0]
        to_mate(index, step).wait_recv()
        total = ins[index][rows_of(owner, rows), :].astype(jnp.float32) + held[index][step].astype(
            jnp.float32
        )
        if not first:
            to_next(index, step - 1).wait_recv()
            total = total + arrived[index][step - 1].astype(jnp.float32)
        held[index][step] = total.astype(jnp.bfloat16)

    for index in range(count):
        add(index, 0, True)
        to_next(index, 0).start()

    def hop(step, carry):
        for index in range(count):
            add(index, step, False)
            to_next(index, step).start()
        return carry

    lax.fori_loop(1, chips - 1, hop, 0)
    for index in range(count):
        add(index, chips - 1, False)
        for shift in range(1, reps):
            to_rep(index, shift).start()
        peers[index][ring.rep] = held[index][chips - 1]
    for index in range(count):
        for shift in range(1, reps):
            to_rep(index, shift).wait_recv()
        total = peers[index][0].astype(jnp.float32)
        for rep in range(1, reps):
            total = total + peers[index][rep].astype(jnp.float32)
        outs[index][...] = total

    def finish(step, carry):
        for index in range(count):
            to_mate(index, step).wait_send()
            pl.when(step < chips - 1)(lambda: to_next(index, step).wait_send())
        return carry

    lax.fori_loop(0, chips, finish, 0)
    for index in range(count):
        for shift in range(1, reps):
            to_rep(index, shift).wait_send()


def scatter_all(pieces, shards, reps):
    chips, count = shards // 2, len(pieces)
    blocks = [(piece.shape[0] // shards, piece.shape[1]) for piece in pieces]
    return pl.pallas_call(
        functools.partial(scatter_kernel, chips, reps, count),
        out_shape=[jax.ShapeDtypeStruct(block, jnp.float32) for block in blocks],
        in_specs=[pl.BlockSpec(memory_space=pltpu.VMEM)] * count,
        out_specs=[pl.BlockSpec(memory_space=pltpu.VMEM)] * count,
        scratch_shapes=[pltpu.VMEM((chips,) + block, jnp.bfloat16) for block in blocks]
        + [pltpu.VMEM((chips - 1,) + block, jnp.bfloat16) for block in blocks]
        + [pltpu.VMEM((reps,) + block, jnp.bfloat16) for block in blocks]
        + [pltpu.SemaphoreType.DMA((chips, count))] * 4
        + [pltpu.SemaphoreType.DMA((reps, count))] * 2,
        compiler_params=pltpu.CompilerParams(
            collective_id=1, has_side_effects=True, vmem_limit_bytes=60 * 1024 * 1024
        ),
        name="scatter_all",
    )(*pieces)


NARROW = (0, 1, 3, 6, 8, 9, 10, 14)
WIDE = 12
WEIGHTS = (2, 4, 5, 7, 11, 13)
LANES = 128
SUBLANES = 16


def packed_rows(size):
    return -(-size // (LANES * SUBLANES)) * SUBLANES


def pack(vectors, owners):
    flat = jnp.concatenate(
        [vectors[i].reshape(owners, -1) for i in NARROW] + [vectors[WIDE].reshape(owners, -1)],
        axis=1,
    )
    rows = packed_rows(flat.shape[1])
    flat = jnp.pad(flat, ((0, 0), (0, rows * LANES - flat.shape[1])))
    return flat.reshape(owners * rows, LANES)


def unpack(block, owners, narrow, wide):
    flat = block.reshape(owners, -1)
    count = len(NARROW)
    first = flat[:, : count * narrow].reshape(owners, count, narrow)
    first = jnp.transpose(first, (1, 0, 2)).reshape(count, owners * narrow)
    found = {i: first[k] for k, i in enumerate(NARROW)}
    found[WIDE] = flat[:, count * narrow : count * narrow + wide].reshape(-1)
    return found


def per_device(shards, reps, frames, cotangent, *local):
    narrow, wide = local[0].shape[0], local[WIDE].shape[0]
    gathered = gather_all([local[i] for i in WEIGHTS] + [pack(local, 1)], shards)
    params = [None] * len(local)
    for k, i in enumerate(WEIGHTS):
        params[i] = gathered[k]
    for i, vector in unpack(gathered[-1], shards, narrow, wide).items():
        params[i] = vector
    params = tuple(params)

    results, input_grads, totals = [], [], None
    for k in range(frames.shape[0]):
        result, saved = forward_clip(frames[k], params)
        d_start, grads = backward_clip(cotangent[k], saved, params)
        results.append(result)
        input_grads.append(d_start)
        totals = grads if totals is None else tuple(a + b for a, b in zip(totals, grads))

    low = [total.astype(jnp.bfloat16) for total in totals]
    summed = scatter_all([low[i] for i in WEIGHTS] + [pack(low, shards)], shards, reps)
    out = [None] * len(local)
    for k, i in enumerate(WEIGHTS):
        out[i] = summed[k]
    for i, vector in unpack(summed[-1], 1, narrow, wide).items():
        out[i] = vector
    return (jnp.stack(results), jnp.stack(input_grads), *out)


def solution(mesh):
    clips = P(("shard", "rep"), None, None)
    weights = tuple(P("shard", None) if i in WEIGHTS else P("shard") for i in range(15))
    return jax.shard_map(
        functools.partial(per_device, mesh.shape["shard"], mesh.shape["rep"]),
        mesh=mesh,
        in_specs=(clips, clips) + weights,
        out_specs=(clips, clips) + weights,
        check_vma=False,
    )
```

time: 807 us -> 264 us (0.33)
  waiting for transfers between devices: 534 us -> 0 us
  Pallas kernels: 0 us -> 170 us
  blocking collectives: 127 us -> 0 us
  other arithmetic: 34.6 us -> 12.2 us
  matrix products: 62.3 us -> 43 us
  between operations: 17.1 us -> 1.27 us
    reduce_scatter x6 -> x0, waiting for transfers between devices: 363 us -> none  [the longest x1 78.5 us: per_device(): lax.psum_scatter(totals[11].astype(jnp.bfloat16), 'shard', scatter_dimens...]
    pallas_call x0 -> x2, Pallas kernels: none -> 170 us  [the longest x1 92.5 us: scatter_all(): pl.pallas_call(functools.partial(scatter_kernel, chips, reps, count), out...]
    all_gather x6 -> x0, waiting for transfers between devices: 167 us -> none  [the longest x1 50.5 us: per_device(): lax.all_gather(inner_weight, 'shard', axis=0, tiled=True)]
    unnamed x2 -> x0, blocking collectives: 121 us -> none
    convert_element_type x22 -> x0, other arithmetic: 22.2 us -> none  [the longest x1 1.81 us: per_device(): lax.psum(shares[11].astype(jnp.bfloat16), 'rep').astype(jnp.float32)]
    dot_general x18, matrix products: 51.4 us -> 35.7 us  [matmul(): return jnp.dot(left, right, preferred_element_type=jnp.float32)]
    unnamed x124 -> x112, local copies, waits for them, and re-layouts: 24.6 us -> 12.5 us
    convert_element_type x2 -> x17, local copies, waits for them, and re-layouts: 0.75 us -> 11.4 us  [the longest x8 7.8 us: per_device(): low = [total.astype(jnp.bfloat16) for total in totals]]
  transfers between devices with their start and end apart: 13 -> 0, of which waited for: 10 -> 0; matrix products, arithmetic and copies ran while one was open for 12% -> 0% of each run, Pallas kernels for 0% -> 0%
where the time goes in v1:
time: 264 us; the launch traced here: 263 us
  Pallas kernels  170 us (64%)
  matrix products  43 us (16%)
  local copies, waits for them, and re-layouts  36.6 us (14%)
  other arithmetic  12.2 us (5%)
    pallas_call x1, Pallas kernels, scatter_all(): pl.pallas_call(functools.partial(scatter_kernel, chips, reps, count), out...  92.5 us
    pallas_call x1, Pallas kernels, gather_all(): pl.pallas_call(functools.partial(gather_kernel, chips, count), out_shape=...  77.6 us
    dot_general x18, matrix products, matmul(): return jnp.dot(left, right, preferred_element_type=jnp.float32)  35.7 us
    unnamed x112, local copies, waits for them, and re-layouts  12.5 us
    convert_element_type x8, local copies, waits for them, and re-layouts, per_device(): low = [total.astype(jnp.bfloat16) for total in totals]  7.8 us

profile of v1, /device:TPU:0, one launch (start us, length us, event | category | flops | bytes accessed | tf_op | source)
XLA Modules:
  0.0 263.3 jit_solution(4524231856505404835)
XLA Ops:
  7.0 77.6 %gather_all.1 = (bf16[768,768]{1,0:T(8,128)(2,1)}, bf16[768,768]{1,0:T(8,128)(2,1)}, bf16[768,768]{1,0:T(8,128)(2,1)}, bf16[768,768]{1,0:T(8,128)(2,1)}, bf16[76...) custom-call(bf16[48,768]{1,0:T(8,128)(2,1)} %refs_0_.1, bf16[48,768]{1,0:T(8,128)(2,1)} %refs_1_.1, ...), custom_call_target="tpu_custom_call" | custom-call | tf_op jit(solution)/shard_map/gather_all/pallas_call | solution.py:331
  89.6 2.0 fusion.10
  95.6 1.9 fusion.60
  100.3 3.7 %multiply_convert_fusion.1 = (bf16[256,3072]{1,0:T(8,128)(2,1)S(1)}, f32[256,3072]{1,0:T(8,128)S(1)}) fusion(f32[3072]{0:T(1024)S(1)} %copy-done.41, bf16[768,3072]{1,0:T(8,128)(2,1)} %get-tuple-element.36, f32[256,768]{1,0:T(8,128)S(1)} %get-tuple-element.78, f32[768]{0:T(1024)S(1)} %copy-done.29, f32[768]{0:T(1024)S(1)} %copy-done.27, ...), kind=kOutput, calls=%fused_computation.11 | convolution fusion | flops 1213661184 | bytes 10244096 | tf_op jit(solution)/shard_map/dot_general | solution.py:46
  104.2 2.9 %fusion.62 = (bf16[3072]{0:T(1024)(128)(2,1)}, bf16[256,3072]{1,0:T(8,128)(2,1)S(1)}) fusion(f32[256,3072]{1,0:T(8,128)S(1)} %get-tuple-element.80, bf16[3072,768]{1,0:T(8,128)(2,1)S(1)} %bitcast.181, bf16[1,256,768]{2,1,0:T(8,128)(2,1)S(1)} %copy-done.10), kind=kOutput, calls=%fused_computation.121 | convolution fusion | flops 1216607232 | bytes 9836544 | tf_op jit(solution)/shard_map/dot_general | solution.py:46
  107.1 2.2 fusion.12
  109.3 3.1 %multiply_reduce_fusion = (bf16[768]{0:T(1024)(128)(2,1)}, f32[256]{0:T(256)}, f32[256]{0:T(256)}, bf16[768]{0:T(1024)(128)(2,1)}, f32[256,768]{1,0:T(8,128)}) fusion(f32[256,768]{1,0:T(8,128)S(1)} %get-tuple-element.78, f32[256]{0:T(256)S(1)} %add_rsqrt_fusion, f32[256]{0:T(256)S(1)} %broadcast_multiply_fusion.4, f32[768]{0:T(1024)S(1)} %copy-done.27, ...), kind=kOutput, calls=%fused_computation.64 | convolution fusion | flops 1209726976 | bytes 7874560 | tf_op jit(solution)/shard_map/dot_general | solution.py:46
  112.4 1.4 convert_element_type.348
  113.8 1.4 convert_element_type.352
  115.9 2.4 fusion.58
  119.2 1.3 convolution_convert_fusion.7
  120.5 1.9 copy.50
  122.4 1.4 convert_element_type.346
  123.8 1.4 convert_element_type.350
  125.1 1.3 multiply_reduce_fusion.1
  126.5 2.3 fusion.59
  133.0 1.4 fusion.27
  136.4 1.7 fusion.39
  138.2 1.5 convolution_convert_fusion.2.refs_3_
  143.0 2.5 convolution_convert_fusion.3.refs_2_
  145.6 2.4 convolution_convert_fusion.4.refs_1_
  147.9 2.4 convolution_convert_fusion.5.refs_0_
  150.4 3.7 %convolution_convert_fusion.1.refs_4_ = bf16[768,3072]{1,0:T(8,128)(2,1)} fusion(bf16[256,3072]{1,0:T(8,128)(2,1)S(1)} %copy-done.19, f32[256,768]{1,0:T(8,128)S(1)} %copy-done.1, f32[768]{0:T(1024)S(1)} %copy-done.30, f32[768]{0:T(1024)S(1)} %copy-done.28, f32[256]{0:T(256)S(1)} %copy-done.40, f32[256]{0:T(256)S(1)} %copy-done.33), kind=kOutput, calls=%fused_computation.1 | convolution fusion | flops 1211301888 | bytes 7086080 | tf_op jit(solution)/shard_map/dot_general | solution.py:46
  154.1 3.8 %convolution_convert_fusion.refs_5_ = bf16[3072,768]{1,0:T(8,128)(2,1)} fusion(bf16[256,3072]{1,0:T(8,128)(2,1)S(1)} %copy-done.13, bf16[1,256,768]{2,1,0:T(8,128)(2,1)S(1)} %copy-done.11), kind=kOutput, calls=%fused_computation | convolution fusion | flops 1210318848 | bytes 6684672 | tf_op jit(solution)/shard_map/dot_general | solution.py:46
  158.0 92.5 %scatter_all.1 = (f32[48,768]{1,0:T(8,128)}, f32[48,768]{1,0:T(8,128)}, f32[48,768]{1,0:T(8,128)}, f32[48,768]{1,0:T(8,128)}, f32[48,3072]{1,0:T(8,128)}, /*index=5*/f32[192,768]{1,0:T(8,128)}, f32[16,128]{1,0:T(8,128)}) custom-call(bf16[768,768]{1,0:T(8,128)(2,1)} %convolution_convert_fusion.5.refs_0_, bf16[768,768]{1,0:T(8,128)(2,1)} %convolution_convert_fusion.4.refs_1_, ...), custom_call_target="tpu_custom_call" | custom-call | tf_op jit(solution)/shard_map/scatter_all/pallas_call | solution.py:452
  251.7 1.4 slice_bitcast_fusion
  253.1 1.6 copy.66
  254.7 1.6 copy.67
  256.3 1.6 copy.68
  257.8 1.6 copy.69
  259.4 1.9 copy.70
  261.3 1.9 copy.71
  (160 shorter events, 30.4 us)
Async XLA Ops:
  1.3 91.3 %copy-start.4 = (bf16[1,256,768]{2,1,0:T(8,128)(2,1)S(1)}, bf16[1,256,768]{2,1,0:T(8,128)(2,1)}, u32[]{:S(2)}) copy-start(bf16[1,256,768]{2,1,0:T(8,128)(2,1)} %param.17) | copy-start | bytes 1179652
  2.5 91.6 %copy-start.42 = (f32[256]{0:T(256)}, f32[256]{0:T(256)S(1)}, u32[]{:S(2)}) copy-start(f32[256]{0:T(256)S(1)} %broadcast_multiply_fusion.5) | copy-start | bytes 3076
  3.8 90.3 %copy-start.44 = (f32[256]{0:T(256)}, f32[256]{0:T(256)S(1)}, u32[]{:S(2)}) copy-start(f32[256]{0:T(256)S(1)} %add_rsqrt_fusion.1) | copy-start | bytes 3076
  84.7 7.9 %copy-start.22 = (bf16[768,768]{1,0:T(8,128)(2,1)S(1)}, bf16[768,768]{1,0:T(8,128)(2,1)}, u32[]{:S(2)}) copy-start(bf16[768,768]{1,0:T(8,128)(2,1)} %get-tuple-element.33) | copy-start | bytes 3538948
  87.4 6.7 %copy-start.34 = (f32[768]{0:T(1024)}, f32[768]{0:T(1024)S(1)}, u32[]{:S(2)}) copy-start(f32[768]{0:T(1024)S(1)} %reshape.388) | copy-start | bytes 9220
  87.5 6.6 %copy-start.46 = (f32[768]{0:T(1024)}, f32[768]{0:T(1024)S(1)}, u32[]{:S(2)}) copy-start(f32[768]{0:T(1024)S(1)} %reshape.389) | copy-start | bytes 9220
  89.6 4.5 %copy-start.20 = (bf16[768,768]{1,0:T(8,128)(2,1)S(1)}, bf16[768,768]{1,0:T(8,128)(2,1)}, u32[]{:S(2)}) copy-start(bf16[768,768]{1,0:T(8,128)(2,1)} %get-tuple-element.34) | copy-start | bytes 3538948
  95.6 8.5 %slice-start.2 = ((s8[4718592]{0:T(1024)(128)(4,1)}), s8[4194304]{0:T(1024)(128)(4,1)S(1)}, s32[]{:S(2)}) async-start(s8[4718592]{0:T(1024)(128)(4,1)} %bitcast.180), calls=%async_computation.2 | async-start | bytes 8388608
  99.4 4.7 %slice-start.3 = ((s8[4718592]{0:T(1024)(128)(4,1)}), s8[524288]{0:T(1024)(128)(4,1)S(1)}, s32[]{:S(2)}) async-start(s8[4718592]{0:T(1024)(128)(4,1)} %bitcast.180), calls=%async_computation.3 | async-start | bytes 1048576
  100.0 9.3 %copy-start = (f32[256,768]{1,0:T(8,128)}, f32[256,768]{1,0:T(8,128)S(1)}, u32[]{:S(2)}) copy-start(f32[256,768]{1,0:T(8,128)S(1)} %get-tuple-element.78) | copy-start | bytes 2359300
  100.0 9.3 %copy-start.32 = (f32[256]{0:T(256)}, f32[256]{0:T(256)S(1)}, u32[]{:S(2)}) copy-start(f32[256]{0:T(256)S(1)} %broadcast_multiply_fusion.4) | copy-start | bytes 3076
  100.3 9.0 %copy-start.39 = (f32[256]{0:T(256)}, f32[256]{0:T(256)S(1)}, u32[]{:S(2)}) copy-start(f32[256]{0:T(256)S(1)} %add_rsqrt_fusion) | copy-start | bytes 3076
  100.3 3.8 %copy-start.10 = (bf16[1,256,768]{2,1,0:T(8,128)(2,1)S(1)}, bf16[1,256,768]{2,1,0:T(8,128)(2,1)}, u32[]{:S(2)}) copy-start(bf16[1,256,768]{2,1,0:T(8,128)(2,1)} %param.18) | copy-start | bytes 1179652
  100.3 9.0 %slice-start = ((s8[4718592]{0:T(1024)(128)(4,1)}), s8[4194304]{0:T(1024)(128)(4,1)S(1)}, s32[]{:S(2)}) async-start(s8[4718592]{0:T(1024)(128)(4,1)} %bitcast.178), calls=%async_computation | async-start | bytes 8388608
  104.2 5.2 %slice-start.1 = ((s8[4718592]{0:T(1024)(128)(4,1)}), s8[524288]{0:T(1024)(128)(4,1)S(1)}, s32[]{:S(2)}) async-start(s8[4718592]{0:T(1024)(128)(4,1)} %bitcast.178), calls=%async_computation.1 | async-start | bytes 1048576
  115.2 4.1 %copy-start.9 = (bf16[768,768]{1,0:T(8,128)(2,1)S(1)}, bf16[768,768]{1,0:T(8,128)(2,1)}, u32[]{:S(2)}) copy-start(bf16[768,768]{1,0:T(8,128)(2,1)} %get-tuple-element.35) | copy-start | bytes 3538948
  125.1 3.6 %copy-start.17 = (bf16[256,768]{0,1:T(8,128)(2,1)S(1)}, bf16[256,768]{0,1:T(8,128)(2,1)}, u32[]{:S(2)}) copy-start(bf16[256,768]{0,1:T(8,128)(2,1)} %copy.46) | copy-start | bytes 1179652
  128.8 4.0 %copy-start.24 = (bf16[256,12,64]{0,2,1:T(8,128)(2,1)}, bf16[256,12,64]{0,2,1:T(8,128)(2,1)S(1)}, u32[]{:S(2)}) copy-start(bf16[256,12,64]{0,2,1:T(8,128)(2,1)S(1)} %get-tuple-element.64) | copy-start | bytes 1179652
  132.2 4.2 %copy-start.3 = (f32[256,768]{1,0:T(8,128)S(1)}, f32[256,768]{1,0:T(8,128)}, u32[]{:S(2)}) copy-start(f32[256,768]{1,0:T(8,128)} %copy-done.2) | copy-start | bytes 2359300
  132.8 5.4 %copy-start.6 = (bf16[12,64,256]{2,1,0:T(8,128)(2,1)S(1)}, bf16[12,64,256]{2,1,0:T(8,128)(2,1)}, u32[]{:S(2)}) copy-start(bf16[12,64,256]{2,1,0:T(8,128)(2,1)} %copy-done.5) | copy-start | bytes 1179652
  134.4 7.1 %copy-start.31 = (bf16[16,192]{1,0:T(8,128)(2,1)S(1)}, bf16[16,192]{1,0:T(8,128)(2,1)}, u32[]{:S(2)}) copy-start(bf16[16,192]{1,0:T(8,128)(2,1)} %convert_element_type.352) | copy-start | bytes 18436
  135.1 6.5 %copy-start.38 = (bf16[16,48]{1,0:T(8,128)(2,1)S(1)}, bf16[16,48]{1,0:T(8,128)(2,1)}, u32[]{:S(2)}) copy-start(bf16[16,48]{1,0:T(8,128)(2,1)} %reshape.384) | copy-start | bytes 4612
  138.2 4.8 %copy-start.25 = (bf16[256,12,64]{0,2,1:T(8,128)(2,1)S(1)}, bf16[256,12,64]{0,2,1:T(8,128)(2,1)}, u32[]{:S(2)}) copy-start(bf16[256,12,64]{0,2,1:T(8,128)(2,1)} %copy-done.24) | copy-start | bytes 1179652
  139.6 8.3 %copy-start.26 = (bf16[256,12,64]{0,2,1:T(8,128)(2,1)S(1)}, bf16[256,12,64]{0,2,1:T(8,128)(2,1)}, u32[]{:S(2)}) copy-start(bf16[256,12,64]{0,2,1:T(8,128)(2,1)} %get-tuple-element.65) | copy-start | bytes 1179652
  143.0 7.4 %copy-start.1 = (f32[256,768]{1,0:T(8,128)S(1)}, f32[256,768]{1,0:T(8,128)}, u32[]{:S(2)}) copy-start(f32[256,768]{1,0:T(8,128)} %copy-done) | copy-start | bytes 2359300
  143.0 7.4 %copy-start.19 = (bf16[256,3072]{1,0:T(8,128)(2,1)S(1)}, bf16[256,3072]{1,0:T(8,128)(2,1)}, u32[]{:S(2)}) copy-start(bf16[256,3072]{1,0:T(8,128)(2,1)} %copy-done.18) | copy-start | bytes 4718596
  143.0 7.4 %copy-start.28 = (f32[768]{0:T(1024)S(1)}, f32[768]{0:T(1024)}, u32[]{:S(2)}) copy-start(f32[768]{0:T(1024)} %reshape.393) | copy-start | bytes 9220
  143.0 7.4 %copy-start.30 = (f32[768]{0:T(1024)S(1)}, f32[768]{0:T(1024)}, u32[]{:S(2)}) copy-start(f32[768]{0:T(1024)} %reshape.394) | copy-start | bytes 9220
  143.0 7.4 %copy-start.33 = (f32[256]{0:T(256)S(1)}, f32[256]{0:T(256)}, u32[]{:S(2)}) copy-start(f32[256]{0:T(256)} %copy-done.32) | copy-start | bytes 3076
  143.0 7.4 %copy-start.40 = (f32[256]{0:T(256)S(1)}, f32[256]{0:T(256)}, u32[]{:S(2)}) copy-start(f32[256]{0:T(256)} %copy-done.39) | copy-start | bytes 3076
  150.4 3.7 %copy-start.11 = (bf16[1,256,768]{2,1,0:T(8,128)(2,1)S(1)}, bf16[1,256,768]{2,1,0:T(8,128)(2,1)}, u32[]{:S(2)}) copy-start(bf16[1,256,768]{2,1,0:T(8,128)(2,1)} %param.18) | copy-start | bytes 1179652
  150.4 3.7 %copy-start.13 = (bf16[256,3072]{1,0:T(8,128)(2,1)S(1)}, bf16[256,3072]{1,0:T(8,128)(2,1)}, u32[]{:S(2)}) copy-start(bf16[256,3072]{1,0:T(8,128)(2,1)} %copy-done.12) | copy-start | bytes 4718596
  (21 other events, 39.8 us)
